TPU v7x, 32 devices: a whole 2x2x4 slice. The times are simulated.
32 devices in a mesh: seq: 16 (over z, y, x), chan: 2 (over core).
Axes of the slice: x: 2, y: 2, z: 4, core: 2. Of those that a mesh axis runs over, the one named last changes fastest.
Arguments:
- inputs: float32 [256, 8192], P('chan', 'seq'), may hold values from -6 to 6
- value_weight: float32 [256, 256], P(None, 'chan'), may hold values from -0.375 to 0.375
- query_weight: float32 [256, 256], P(None, 'chan'), may hold values from -0.375 to 0.375
- filters: float32 [256, 8192], P('chan', 'seq'), may hold values from -1 to 1
- grad_out: float32 [256, 8192], P('chan', 'seq'), may hold values from -6 to 6
Outputs:
- input_grad: float32 [256, 8192], P('chan', 'seq')
- filter_grad: float32 [256, 8192], P('chan', 'seq')
- value_gradient: float32 [256, 256], P(None, 'chan')
- query_gradient: float32 [256, 256], P(None, 'chan')
All inputs are finite; a program needn't handle non-finite values.
Results may differ from a plain program's by a relative error of at most 0.00018.
Values sent between devices are 32-bit elements; how exact they have to be, the bound alone decides.
A program may use at most 64 MiB of HBM per device.

v0:
```python
import math

import jax
import jax.numpy as jnp
from jax import lax
from jax.sharding import PartitionSpec as P

BLK = 64


HIGHEST = lax.Precision.HIGHEST


def complex_table(row_count, col_count, period, direction):
    row_iota = lax.broadcasted_iota(jnp.int32, (row_count, col_count), 0)
    col_iota = lax.broadcasted_iota(jnp.int32, (row_count, col_count), 1)
    rotation = 2.0 * math.pi / period * (row_iota * col_iota % period).astype(jnp.float32)
    cosine = jnp.cos(rotation)
    sine_part = direction * jnp.sin(rotation)
    upper_rows = jnp.stack([cosine, sine_part], axis=1)
    lower_rows = jnp.stack([-sine_part, cosine], axis=1)
    return jnp.stack([upper_rows, lower_rows], axis=0)


def rotate(columns, cosine, sine_part):
    return jnp.stack(
        [columns[0] * cosine - columns[1] * sine_part, columns[0] * sine_part + columns[1] * cosine]
    )


def multiply(first_spec, second_spec, conjugate):
    imag_first = -first_spec[1] if conjugate else first_spec[1]
    return jnp.stack(
        [
            first_spec[0] * second_spec[0] - imag_first * second_spec[1],
            first_spec[0] * second_spec[1] + imag_first * second_spec[0],
        ]
    )


def block_angles(block_size, inner_size, seq_rows, direction):
    outer_iota = lax.broadcasted_iota(jnp.int32, (block_size, inner_size), 0)
    inner_iota = lax.broadcasted_iota(jnp.int32, (block_size, inner_size), 1)
    rotation = (
        direction
        * 2.0
        * math.pi
        / seq_rows
        * (outer_iota * inner_iota % seq_rows).astype(jnp.float32)
    )
    return (jnp.cos(rotation)[:, :, None], jnp.sin(rotation)[:, :, None])


def local_forward(columns, block_size):
    seq_rows = columns.shape[1]
    item_width = columns.shape[2]
    inner_size = seq_rows // block_size
    shaped = columns.reshape(2, block_size, inner_size, item_width)
    first_pass = jnp.einsum(
        "xabz,xayk->ykbz",
        shaped,
        complex_table(block_size, block_size, block_size, -1.0),
        precision=HIGHEST,
    )
    cosine, sine_part = block_angles(block_size, inner_size, seq_rows, -1.0)
    rotated = rotate(first_pass, cosine, sine_part)
    second = jnp.einsum(
        "ykbz,ybwm->wkmz",
        rotated,
        complex_table(inner_size, inner_size, inner_size, -1.0),
        precision=HIGHEST,
    )
    return second.reshape(2, seq_rows, item_width)


def local_inverse(columns, block_size):
    seq_rows = columns.shape[1]
    item_width = columns.shape[2]
    inner_size = seq_rows // block_size
    shaped = columns.reshape(2, block_size, inner_size, item_width)
    first_pass = jnp.einsum(
        "xkmz,xmyb->ykbz",
        shaped,
        complex_table(inner_size, inner_size, inner_size, 1.0),
        precision=HIGHEST,
    )
    cosine, sine_part = block_angles(block_size, inner_size, seq_rows, 1.0)
    rotated = rotate(first_pass, cosine, sine_part)
    second = jnp.einsum(
        "xkbz,xkya->yabz",
        rotated,
        complex_table(block_size, block_size, block_size, 1.0),
        precision=HIGHEST,
    )
    return second.reshape(2, seq_rows, item_width) * (1.0 / seq_rows)


def cross_transform(columns, dft_table):
    seq_rows = columns.shape[1]
    item_width = columns.shape[2]
    shaped = columns.reshape(2, 1, seq_rows, item_width)
    transformed = jnp.einsum(
        "xpjz,xpyk->ykjz",
        lax.all_to_all(shaped, "seq", split_axis=2, concat_axis=1, tiled=True),
        dft_table,
        precision=HIGHEST,
    )
    result = lax.all_to_all(transformed, "seq", split_axis=1, concat_axis=2, tiled=True)
    return result.reshape(2, seq_rows, item_width)


def shard_twiddle(columns, frequency, seq_length, direction):
    seq_rows = columns.shape[1]
    local_pos = jnp.arange(seq_rows, dtype=jnp.int32)
    rotation = (
        direction
        * 2.0
        * math.pi
        / seq_length
        * (local_pos * frequency % seq_length).astype(jnp.float32)
    )
    return rotate(columns, jnp.cos(rotation)[:, None], jnp.sin(rotation)[:, None])


def forward(columns, shard_index, devices, block_size):
    seq_length = columns.shape[1] * devices
    columns = cross_transform(columns, complex_table(devices, devices, devices, -1.0))
    columns = shard_twiddle(columns, shard_index, seq_length, -1.0)
    return local_forward(columns, block_size)


def inverse(columns, shard_index, devices, block_size):
    seq_length = columns.shape[1] * devices
    columns = local_inverse(columns, block_size)
    columns = shard_twiddle(columns, shard_index, seq_length, 1.0)
    columns = cross_transform(
        columns, complex_table(devices, devices, devices, 1.0) * (1.0 / devices)
    )
    return columns


def per_device(inputs, value_weight, query_weight, filters, grad_out):
    channel_count = filters.shape[0]
    seq_rows = filters.shape[1]
    devices = lax.axis_size("seq")
    shard_index = lax.axis_index("seq")
    seq_length = seq_rows * devices
    grad_scale = 1.0 / math.sqrt(seq_length)
    all_inputs = lax.all_gather(inputs, "chan", axis=0, tiled=True)
    projected = jnp.einsum("cd,ct->dt", value_weight, all_inputs, precision=HIGHEST)
    query_proj = jnp.einsum("cd,ct->dt", query_weight, all_inputs, precision=HIGHEST)
    gated_grad = grad_out * query_proj
    signals = jnp.stack([projected, filters, gated_grad])
    position = shard_index * seq_rows + jnp.arange(seq_rows, dtype=jnp.int32)
    twist_angle = 0.5 * math.pi / seq_length * position.astype(jnp.float32)
    cosine = jnp.cos(twist_angle)
    sine_part = jnp.sin(twist_angle)
    twisted = jnp.stack([signals * cosine, -signals * sine_part])
    columns = jnp.transpose(twisted, (0, 3, 1, 2)).reshape(2, seq_rows, 3 * channel_count)
    spectra = forward(columns, shard_index, devices, BLK).reshape(2, seq_rows, 3, channel_count)
    value_spec = spectra[:, :, 0]
    filter_spec = spectra[:, :, 1]
    grad_spec = spectra[:, :, 2]
    products = jnp.stack(
        [
            multiply(filter_spec, value_spec, False),
            multiply(filter_spec, grad_spec, True),
            multiply(value_spec, grad_spec, True),
        ],
        axis=2,
    )
    restored = inverse(
        products.reshape(2, seq_rows, 3 * channel_count), shard_index, devices, BLK
    ).reshape(2, seq_rows, 3, channel_count)
    combined = restored[0] * cosine[:, None, None] - restored[1] * sine_part[:, None, None]
    combined = jnp.transpose(combined, (1, 2, 0))
    convolved = combined[0]
    grad_value = combined[1]
    filter_grad = combined[2] * grad_scale
    grad_query = grad_out * convolved
    input_grad = lax.psum_scatter(
        jnp.dot(value_weight, grad_value, precision=HIGHEST, preferred_element_type=jnp.float32)
        + jnp.dot(query_weight, grad_query, precision=HIGHEST, preferred_element_type=jnp.float32),
        "chan",
        scatter_dimension=0,
        tiled=True,
    )
    partial_value = jnp.einsum("ct,dt->cd", all_inputs, grad_value, precision=HIGHEST) * grad_scale
    partial_query = jnp.einsum("ct,dt->cd", all_inputs, grad_query, precision=HIGHEST) * grad_scale
    value_gradient, query_gradient = lax.psum((partial_value, partial_query), "seq")
    return (input_grad, filter_grad, value_gradient, query_gradient)


def solution(mesh):
    return jax.shard_map(
        per_device,
        mesh=mesh,
        in_specs=(
            P("chan", "seq"),
            P(None, "chan"),
            P(None, "chan"),
            P("chan", "seq"),
            P("chan", "seq"),
        ),
        out_specs=(P("chan", "seq"), P("chan", "seq"), P(None, "chan"), P(None, "chan")),
        check_vma=False,
    )
```

profile of v0, /device:TPU:0, one launch (start us, length us, event | category | flops | bytes accessed | tf_op | source)
XLA Modules:
  0.0 338.8 jit_solution(11861713930455157449)
XLA Ops:
  8.1 2.6 all_gather.3
  10.7 0.5 convolution_bitcast_fusion
  11.2 0.5 fusion.34
  11.7 0.2 fusion.39
  11.9 0.2 pad_maximum_fusion
  12.1 2.2 copy.72
  14.3 8.2 %all-to-all-start = ((f32[2,1,512,384]{3,0,1,2:T(2,128)}), f32[2,1,512,384]{3,0,1,2:T(2,128)S(1)}, u32[]{:S(2)}, u32[]{:S(2)}) async-start(f32[2,1,512,384]{3,0,1,2:T(2,128)} %copy.72), calls=%async_computation | async-start | bytes 3145728 | tf_op jit(solution)/shard_map/all_to_all | solution.py:104
  22.8 34.0 %all-to-all-done = f32[2,1,512,384]{3,0,1,2:T(2,128)S(1)} async-done(((f32[2,1,512,384]{3,0,1,2:T(2,128)}), f32[2,1,512,384]{3,0,1,2:T(2,128)S(1)}, u32[]{:S(2)}, u32[]{:S(2)}) %all-to-all-start) | async-done | bytes 1572896 | tf_op jit(solution)/shard_map/all_to_all | solution.py:104
  56.8 2.3 fusion.18
  59.1 1.7 copy.75
  60.8 8.1 %all-to-all-start.1 = ((f32[2,16,32,384]{3,2,0,1:T(8,128)}), f32[2,16,32,384]{3,2,0,1:T(8,128)S(1)}, u32[]{:S(2)}, u32[]{:S(2)}) async-start(f32[2,16,32,384]{3,2,0,1:T(8,128)} %copy.75), calls=%async_computation.1 | async-start | bytes 3145728 | tf_op jit(solution)/shard_map/all_to_all | solution.py:108
  69.9 0.1 broadcast_multiply_fusion
  70.1 0.1 fusion.68
  70.3 32.0 %all-to-all-done.1 = f32[2,16,32,384]{3,2,0,1:T(8,128)S(1)} async-done(((f32[2,16,32,384]{3,2,0,1:T(8,128)}), f32[2,16,32,384]{3,2,0,1:T(8,128)S(1)}, u32[]{:S(2)}, u32[]{:S(2)}) %all-to-all-start.1) | async-done | bytes 1572896 | tf_op jit(solution)/shard_map/all_to_all | solution.py:108
  102.4 0.3 multiply_subtract_fusion.2
  102.7 1.5 fusion.32
  104.2 0.2 multiply_subtract_fusion.1
  104.6 3.4 fusion.21
  108.0 2.5 reshape_reshape.11
  110.5 1.1 fusion.116
  111.6 0.2 multiply_subtract_fusion.5
  112.0 1.1 copy.88
  113.1 1.8 reshape_reshape.12
  114.9 2.9 fusion.24
  117.8 0.2 multiply_subtract_fusion
  118.1 1.6 bitcast_multiply_fusion
  119.9 0.9 fusion.37
  120.9 1.2 copy.96
  122.2 44.1 %all_to_all.42 = f32[2,1,512,384]{3,0,1,2:T(2,128)S(1)} all-to-all(f32[2,1,512,384]{3,0,1,2:T(2,128)S(1)} %copy.96), channel_id=1, replica_groups=mesh['seq'=16,'chan'=2] {'seq'}, dimensions={2} | all-to-all | bytes 3145728 | tf_op jit(solution)/shard_map/all_to_all | solution.py:104
  166.3 2.3 fusion.29
  168.5 1.7 copy.100
  170.2 4.0 %all-to-all-start.3 = ((f32[2,16,32,384]{3,2,0,1:T(8,128)}), f32[2,16,32,384]{3,2,0,1:T(8,128)S(1)}, u32[]{:S(2)}, u32[]{:S(2)}) async-start(f32[2,16,32,384]{3,2,0,1:T(8,128)} %copy.100), calls=%async_computation.3 | async-start | bytes 3145728 | tf_op jit(solution)/shard_map/all_to_all | solution.py:108
  174.2 0.8 copy.101
  175.1 32.6 %all-to-all-done.3 = f32[2,16,32,384]{3,2,0,1:T(8,128)S(1)} async-done(((f32[2,16,32,384]{3,2,0,1:T(8,128)}), f32[2,16,32,384]{3,2,0,1:T(8,128)S(1)}, u32[]{:S(2)}, u32[]{:S(2)}) %all-to-all-start.3) | async-done | bytes 1572896 | tf_op jit(solution)/shard_map/all_to_all | solution.py:108
  207.7 1.0 fusion.117
  208.7 1.4 squeeze.32
  210.1 0.3 squeeze.33
  210.5 1.9 subtract_bitcast_fusion
  212.4 0.6 slice_multiply_fusion
  213.0 1.3 fusion.36
  214.3 0.6 fusion.120
  214.9 1.3 fusion.35
  216.2 1.4 fusion.33
  217.6 0.8 copy.103
  218.5 107.8 %all-reduce.3.cloned.1.call-done = (f32[256,128]{0,1:T(8,128)}, f32[256,128]{0,1:T(8,128)}) async-done(((f32[256,128]{0,1:T(8,128)}, f32[256,128]{0,1:T(8,128)}), (f32[256,128]{0,1:T(8,128)}, f32[256,128]{0,1:T(8,128)})) %all-reduce.3.cloned.1.call-update) | async-done | bytes 262160 | tf_op jit(solution)/shard_map/psum | solution.py:190
  326.2 1.7 copy.104
  327.9 1.7 copy.105
  329.5 1.8 copy.102
  (48 shorter events, 2.2 us)
Async XLA Ops:
  8.0 2.7 copy-start
  8.0 3.2 copy-start.3
  8.0 3.2 copy-start.2
  8.0 3.7 %copy-start.5 = (f32[128,512]{1,0:T(8,128)S(1)}, f32[128,512]{1,0:T(8,128)}, u32[]{:S(2)}) copy-start(f32[128,512]{1,0:T(8,128)} %param.8) | copy-start | bytes 786436
  14.3 42.5 %all-to-all-start = ((f32[2,1,512,384]{3,0,1,2:T(2,128)}), f32[2,1,512,384]{3,0,1,2:T(2,128)S(1)}, u32[]{:S(2)}, u32[]{:S(2)}) async-start(f32[2,1,512,384]{3,0,1,2:T(2,128)} %copy.72), calls=%async_computation | async-start | bytes 3145728 | tf_op jit(solution)/shard_map/all_to_all | solution.py:104
  60.8 41.5 %all-to-all-start.1 = ((f32[2,16,32,384]{3,2,0,1:T(8,128)}), f32[2,16,32,384]{3,2,0,1:T(8,128)S(1)}, u32[]{:S(2)}, u32[]{:S(2)}) async-start(f32[2,16,32,384]{3,2,0,1:T(8,128)} %copy.75), calls=%async_computation.1 | async-start | bytes 3145728 | tf_op jit(solution)/shard_map/all_to_all | solution.py:108
  170.2 37.5 %all-to-all-start.3 = ((f32[2,16,32,384]{3,2,0,1:T(8,128)}), f32[2,16,32,384]{3,2,0,1:T(8,128)S(1)}, u32[]{:S(2)}, u32[]{:S(2)}) async-start(f32[2,16,32,384]{3,2,0,1:T(8,128)} %copy.100), calls=%async_computation.3 | async-start | bytes 3145728 | tf_op jit(solution)/shard_map/all_to_all | solution.py:108
  174.2 152.0 %all-reduce.3.cloned.1.call-start = ((), (), s32[]{:S(2)}) async-start(), calls=%async_computation.6 | async-start | bytes 524288 | tf_op jit(solution)/shard_map/psum | solution.py:190
  212.3 2.5 copy-start.1
  213.0 3.2 copy-start.4
  216.2 113.4 %reduce-scatter.2.cloned.1.call-start = ((), (), s32[]{:S(2)}) async-start(), calls=%async_computation.5 | async-start | bytes 786432 | tf_op jit(solution)/shard_map/reduce_scatter | solution.py:181
Sparse Core Ops, SparseCore 0:
  216.3 109.9 all-reduce.2
Sparse Core Ops, SparseCore 1:
  218.9 9.6 reduce-scatter.1
where the time goes:
time: 339 us
  waiting for transfers between devices  206 us (61%)
  blocking collectives  46.7 us (14%)
  local copies, waits for them, and re-layouts  23.5 us (7%)
  starting transfers between devices  20.3 us (6%)
  matrix products  19.4 us (6%)
  between operations  15.9 us (5%)
  other arithmetic  6.45 us (2%)
    psum x1, waiting for transfers between devices, per_device(): lax.psum((partial_value, partial_query), 'seq')  108 us
    all_to_all x2, waiting for transfers between devices, cross_transform(): lax.all_to_all(transformed, 'seq', split_axis=1, concat_axis=2, tiled=True)  64.6 us
    all_to_all x1, blocking collectives, cross_transform(): lax.all_to_all(shaped, 'seq', split_axis=2, concat_axis=1, tiled=True)  44.1 us
    all_to_all x1, waiting for transfers between devices, cross_transform(): lax.all_to_all(shaped, 'seq', split_axis=2, concat_axis=1, tiled=True)  34 us
    all_to_all x2, starting transfers between devices, cross_transform(): lax.all_to_all(transformed, 'seq', split_axis=1, concat_axis=2, tiled=True)  12 us
    all_to_all x1, starting transfers between devices, cross_transform(): lax.all_to_all(shaped, 'seq', split_axis=2, concat_axis=1, tiled=True)  8.22 us
    unnamed x17, local copies, waits for them, and re-layouts  6.81 us
  transfers between devices with their start and end apart: 5, of which 4 were waited for; matrix products, arithmetic and copies ran while one was open for 2% of the time, Pallas kernels for 0%

commit v1 on v0

--- a/solution.py
+++ b/solution.py
@@ -1,11 +1,17 @@
+import functools
 import math
 
 import jax
 import jax.numpy as jnp
+import numpy as np
 from jax import lax
+from jax.experimental import pallas as pl
+from jax.experimental.pallas import tpu as pltpu
 from jax.sharding import PartitionSpec as P
 
 BLK = 64
+LANES = 128
+GROUP = 8
 
 
 HIGHEST = lax.Precision.HIGHEST
@@ -191,9 +197,363 @@
     return (input_grad, filter_grad, value_gradient, query_gradient)
 
 
+NN = (((1,), (0,)), ((), ()))
+NT = (((1,), (1,)), ((), ()))
+
+
+def split_table(table):
+    high = table.astype(jnp.bfloat16)
+    low = (table - high.astype(np.float32)).astype(jnp.bfloat16)
+    return high, low
+
+
+@functools.lru_cache(maxsize=None)
+def transform_tables(seq_length):
+    outer = seq_length // LANES
+    k = np.arange(outer, dtype=np.float64)
+    a = np.arange(outer, dtype=np.float64)
+    b = np.arange(LANES, dtype=np.float64)
+    phase = 2 * np.pi * np.outer(4 * k + 1, a) % (2 * np.pi * 4 * outer) / (4 * outer)
+    small = np.concatenate([np.cos(phase), -np.sin(phase)], axis=0)
+    wide = np.kron(small, np.eye(GROUP)).astype(np.float32)
+    angle = 2 * np.pi * np.repeat(np.outer(4 * k + 1, b), GROUP, axis=0) / (4 * seq_length)
+    turn = np.stack([np.cos(angle), np.sin(angle)]).astype(np.float32)
+    inner = 2 * np.pi * (np.outer(b, b) % LANES) / LANES
+    c, s = np.cos(inner), np.sin(inner)
+    ahead = np.block([[c, -s], [s, c]]).astype(np.float32)
+    back = np.block([[c, s], [-s, c]]).astype(np.float32)
+    return (
+        *split_table(wide),
+        *split_table(np.ascontiguousarray(wide.T) / np.float32(seq_length)),
+        *split_table(ahead),
+        *split_table(back),
+        turn,
+    )
+
+
+def split(x):
+    high = x.astype(jnp.bfloat16)
+    return high, (x - high.astype(jnp.float32)).astype(jnp.bfloat16)
+
+
+def dot3(first, second, dims=NN):
+    def dot(x, y):
+        return lax.dot_general(x, y, dims, preferred_element_type=jnp.float32)
+
+    return dot(first[0], second[0]) + (dot(first[0], second[1]) + dot(first[1], second[0]))
+
+
+def fused_kernel(
+    devices,
+    scale,
+    x_ref,
+    vw_ref,
+    qw_ref,
+    f_ref,
+    g_ref,
+    wide_h,
+    wide_l,
+    tall_h,
+    tall_l,
+    ahead_h,
+    ahead_l,
+    back_h,
+    back_l,
+    turn_ref,
+    ig_out,
+    fg_out,
+    vg_out,
+    qg_out,
+    other_x,
+    out_block,
+    send_sig,
+    in_sig,
+    spec,
+    out_sig,
+    ret_sig,
+    part,
+    scat,
+    red,
+    gath,
+    ig_send,
+    ig_recv,
+    ssem,
+    rsem,
+    csend,
+    crecv,
+):
+    me = lax.axis_index("seq")
+    chan = lax.axis_index("chan")
+    half, width = x_ref.shape
+    pieces = width // LANES
+    rows = 2 * half // devices
+
+    barrier = pltpu.get_barrier_semaphore()
+
+    def greet(i, carry):
+        pl.semaphore_signal(
+            barrier,
+            inc=1,
+            device_id={"seq": lax.rem(me + i, devices)},
+            device_id_type=pl.DeviceIdType.MESH,
+        )
+        return carry
+
+    lax.fori_loop(1, devices, greet, 0)
+    pl.semaphore_signal(
+        barrier, inc=1, device_id={"chan": 1 - chan}, device_id_type=pl.DeviceIdType.MESH
+    )
+
+    own_rows = pl.ds(pl.multiple_of(chan * half, half), half)
+    other_rows = pl.ds(pl.multiple_of((1 - chan) * half, half), half)
+    own_x = split(x_ref[...])
+    partial_value = dot3(split(vw_ref[own_rows, :].T), own_x)
+    partial_query = dot3(split(qw_ref[own_rows, :].T), own_x)
+
+    pl.semaphore_wait(barrier, devices)
+
+    def exchange(index, src, dst):
+        return pltpu.make_async_remote_copy(
+            src_ref=src,
+            dst_ref=dst,
+            send_sem=csend.at[index],
+            recv_sem=crecv.at[index],
+            device_id={"chan": 1 - chan},
+            device_id_type=pl.DeviceIdType.MESH,
+        )
+
+    def each(slot, src_of, dst_of, what):
+        def step(i, carry):
+            peer = lax.rem(me + i, devices)
+            copy = pltpu.make_async_remote_copy(
+                src_ref=src_of(peer),
+                dst_ref=dst_of(),
+                send_sem=ssem.at[slot, i],
+                recv_sem=rsem.at[slot, i],
+                device_id={"seq": peer},
+                device_id_type=pl.DeviceIdType.MESH,
+            )
+            getattr(copy, what)()
+            return carry
+
+        lax.fori_loop(1, devices, step, 0)
+
+    def group_rows(peer, count):
+        return pl.ds(pl.multiple_of(peer * count, count), count)
+
+    def out_way(slot, what):
+        src = f_ref if slot == 0 else send_sig.at[slot - 1]
+        each(slot, lambda p: src.at[group_rows(p, GROUP), :], lambda: in_sig.at[slot, me], what)
+
+    def back_way(slot, what):
+        each(
+            3 + slot,
+            lambda p: out_sig.at[slot, p],
+            lambda: ret_sig.at[slot, group_rows(me, GROUP), :],
+            what,
+        )
+
+    def scatter(slot, what):
+        each(
+            6 + slot,
+            lambda p: part.at[slot, group_rows(p, rows), :],
+            lambda: scat.at[slot, me],
+            what,
+        )
+
+    def gather(slot, what):
+        each(
+            8 + slot,
+            lambda p: red.at[slot],
+            lambda: gath.at[slot, group_rows(me, rows), :],
+            what,
+        )
+
+    give_x = exchange(0, x_ref, other_x)
+    give_x.start()
+    out_way(0, "start")
+    in_sig[0, me] = f_ref[group_rows(me, GROUP), :]
+    give_x.wait()
+
+    far_x = split(other_x[...])
+    send_sig[0] = partial_value + dot3(split(vw_ref[other_rows, :].T), far_x)
+    out_way(1, "start")
+    in_sig[1, me] = send_sig[0, group_rows(me, GROUP), :]
+    query_proj = partial_query + dot3(split(qw_ref[other_rows, :].T), far_x)
+    send_sig[1] = g_ref[...] * query_proj
+    out_way(2, "start")
+    in_sig[2, me] = send_sig[1, group_rows(me, GROUP), :]
+
+    wide = (wide_h[...], wide_l[...])
+    tall = (tall_h[...], tall_l[...])
+    ahead = (ahead_h[...], ahead_l[...])
+    back = (back_h[...], back_l[...])
+    cosine = turn_ref[0]
+    sine = turn_ref[1]
+    count = cosine.shape[0]
+
+    def transform(slot):
+        signal = jnp.concatenate(
+            [
+                in_sig[slot, source, :, piece * LANES : (piece + 1) * LANES]
+                for source in range(devices)
+                for piece in range(pieces)
+            ],
+            axis=0,
+        )
+        first = dot3(wide, split(signal))
+        real, imag = first[:count], first[count:]
+        turned = jnp.concatenate(
+            [real * cosine + imag * sine, imag * cosine - real * sine], axis=1
+        )
+        spec[slot] = dot3(split(turned), ahead)
+
+    def restore(first, second, conjugate, slot):
+        real_a, imag_a = spec[first, :, :LANES], spec[first, :, LANES:]
+        real_b, imag_b = spec[second, :, :LANES], spec[second, :, LANES:]
+        if conjugate:
+            imag_a = -imag_a
+        product = jnp.concatenate(
+            [real_a * real_b - imag_a * imag_b, real_a * imag_b + imag_a * real_b], axis=1
+        )
+        inner = dot3(split(product), back)
+        real, imag = inner[:, :LANES], inner[:, LANES:]
+        turned = jnp.concatenate(
+            [real * cosine - imag * sine, imag * cosine + real * sine], axis=0
+        )
+        signal = dot3(tall, split(turned))
+        for target in range(devices):
+            for piece in range(pieces):
+                at = (target * pieces + piece) * GROUP
+                out_sig[slot, target, :, piece * LANES : (piece + 1) * LANES] = signal[
+                    at : at + GROUP
+                ]
+        back_way(slot, "start")
+        ret_sig[slot, group_rows(me, GROUP), :] = out_sig[slot, me]
+
+    out_way(0, "wait_recv")
+    transform(0)
+    out_way(1, "wait_recv")
+    transform(1)
+    restore(0, 1, False, 0)
+    out_way(2, "wait_recv")
+    transform(2)
+    restore(0, 2, True, 1)
+    restore(1, 2, True, 2)
+
+    def weight_part(slot, grad):
+        near = dot3(own_x2, grad, NT)
+        far = dot3(far_x2, grad, NT)
+        part[slot, own_rows, :] = near
+        part[slot, other_rows, :] = far
+        scatter(slot, "start")
+        scat[slot, me] = part[slot, group_rows(me, rows), :]
+
+    own_x2 = split(x_ref[...])
+    far_x2 = split(other_x[...])
+    back_way(0, "wait_recv")
+    grad_query = split(g_ref[...] * ret_sig[0])
+    weight_part(0, grad_query)
+    near_grad = dot3(split(qw_ref[own_rows, :]), grad_query)
+    far_grad = dot3(split(qw_ref[other_rows, :]), grad_query)
+    back_way(1, "wait_recv")
+    grad_value = split(ret_sig[1])
+    ig_send[...] = far_grad + dot3(split(vw_ref[other_rows, :]), grad_value)
+    give_ig = exchange(1, ig_send, ig_recv)
+    give_ig.start()
+    weight_part(1, grad_value)
+
+    def reduce(slot):
+        scatter(slot, "wait_recv")
+        total = scat[slot, 0]
+        for source in range(1, devices):
+            total = total + scat[slot, source]
+        red[slot] = total * scale
+        gather(slot, "start")
+        gath[slot, group_rows(me, rows), :] = red[slot]
+
+    reduce(0)
+    near_grad = near_grad + dot3(split(vw_ref[own_rows, :]), grad_value)
+    reduce(1)
+    give_ig.wait()
+    ig_out[...] = near_grad + ig_recv[...]
+    back_way(2, "wait_recv")
+    fg_out[...] = ret_sig[2] * scale
+    for slot, out in ((0, qg_out), (1, vg_out)):
+        gather(slot, "wait_recv")
+        out[...] = gath[slot]
+    for slot in range(3):
+        out_way(slot, "wait_send")
+        back_way(slot, "wait_send")
+    for slot in range(2):
+        scatter(slot, "wait_send")
+        gather(slot, "wait_send")
+
+
+def fused_device(inputs, value_weight, query_weight, filters, grad_out):
+    half, width = inputs.shape
+    devices = lax.axis_size("seq")
+    seq_length = width * devices
+    depth = value_weight.shape[0]
+    rows = depth // devices
+    tables = transform_tables(seq_length)
+    count = seq_length // LANES * GROUP
+    vmem = pl.BlockSpec(memory_space=pltpu.VMEM)
+    f32 = jnp.float32
+    ig, fg, vg, qg = pl.pallas_call(
+        functools.partial(fused_kernel, devices, 1.0 / math.sqrt(seq_length)),
+        out_shape=(
+            jax.ShapeDtypeStruct((half, width), f32),
+            jax.ShapeDtypeStruct((half, width), f32),
+            jax.ShapeDtypeStruct((depth, half), f32),
+            jax.ShapeDtypeStruct((depth, half), f32),
+        ),
+        in_specs=[vmem] * (5 + len(tables)),
+        out_specs=(vmem,) * 4,
+        scratch_shapes=[
+            pltpu.VMEM((half, width), f32),
+            pltpu.VMEM((GROUP, LANES), f32),
+            pltpu.VMEM((2, half, width), f32),
+            pltpu.VMEM((3, devices, GROUP, width), f32),
+            pltpu.VMEM((3, count, 2 * LANES), f32),
+            pltpu.VMEM((3, devices, GROUP, width), f32),
+            pltpu.VMEM((3, half, width), f32),
+            pltpu.VMEM((2, depth, half), f32),
+            pltpu.VMEM((2, devices, rows, half), f32),
+            pltpu.VMEM((2, rows, half), f32),
+            pltpu.VMEM((2, depth, half), f32),
+            pltpu.VMEM((half, width), f32),
+            pltpu.VMEM((half, width), f32),
+            pltpu.SemaphoreType.DMA((10, devices)),
+            pltpu.SemaphoreType.DMA((10, devices)),
+            pltpu.SemaphoreType.DMA((2,)),
+            pltpu.SemaphoreType.DMA((2,)),
+        ],
+        compiler_params=pltpu.CompilerParams(
+            collective_id=0, has_side_effects=True, vmem_limit_bytes=56 * 1024 * 1024
+        ),
+    )(inputs, value_weight, query_weight, filters, grad_out, *(jnp.asarray(t) for t in tables))
+    return ig, fg, vg, qg
+
+
+def on_device(inputs, value_weight, query_weight, filters, grad_out):
+    channel_count, width = filters.shape
+    devices = lax.axis_size("seq")
+    fits = (
+        channel_count == GROUP * devices
+        and channel_count == inputs.shape[0]
+        and lax.axis_size("chan") == 2
+        and width % LANES == 0
+        and channel_count % LANES == 0
+        and value_weight.shape[0] % (GROUP * devices) == 0
+    )
+    body = fused_device if fits else per_device
+    return body(inputs, value_weight, query_weight, filters, grad_out)
+
+
 def solution(mesh):
     return jax.shard_map(
-        per_device,
+        on_device,
         mesh=mesh,
         in_specs=(
             P("chan", "seq"),

time: 339 us -> 72 us (0.21)
  waiting for transfers between devices: 206 us -> 0 us
  Pallas kernels: 0 us -> 66.9 us
  blocking collectives: 46.7 us -> 0 us
  starting transfers between devices: 20.3 us -> 0 us
  matrix products: 19.4 us -> 0 us
  local copies, waits for them, and re-layouts: 23.5 us -> 4.32 us
  between operations: 15.9 us -> 0.65 us
  other arithmetic: 6.45 us -> 0 us
    psum x1 -> x0, waiting for transfers between devices: 108 us -> none  [per_device(): lax.psum((partial_value, partial_query), 'seq')]
    all_to_all x3 -> x0, waiting for transfers between devices: 98.7 us -> none  [the longest x2 64.6 us: cross_transform(): lax.all_to_all(transformed, 'seq', split_axis=1, concat_axis=2, tiled=True)]
    pallas_call x0 -> x1, Pallas kernels: none -> 66.9 us  [fused_device(): pl.pallas_call(functools.partial(fused_kernel, devices, 1.0 / math.sqrt(s...]
    all_to_all x1 -> x0, blocking collectives: 44.1 us -> none  [cross_transform(): lax.all_to_all(shaped, 'seq', split_axis=2, concat_axis=1, tiled=True)]
    all_to_all x3 -> x0, starting transfers between devices: 20.2 us -> none  [the longest x2 12 us: cross_transform(): lax.all_to_all(transformed, 'seq', split_axis=1, concat_axis=2, tiled=True)]
    dot_general x12 -> x0, matrix products: 19.4 us -> none  [the longest x2 4.56 us: cross_transform(): jnp.einsum('xpjz,xpyk->ykjz', lax.all_to_all(shaped, 'seq', split_axis=2,...]
    another operation x8 -> x0, local copies, waits for them, and re-layouts: 7.86 us -> none  [the longest x1 2.49 us: per_device(): forward(columns, shard_index, devices, BLK)]
    unnamed x17 -> x10, local copies, waits for them, and re-layouts: 6.81 us -> 4.32 us
  transfers between devices with their start and end apart: 5 -> 0, of which waited for: 4 -> 0; matrix products, arithmetic and copies ran while one was open for 2% -> 0% of each run, Pallas kernels for 0% -> 0%
where the time goes in v1:
time: 72 us; the launch traced here: 71.9 us
  Pallas kernels  66.9 us (93%)
  local copies, waits for them, and re-layouts  4.32 us (6%)
    pallas_call x1, Pallas kernels, fused_device(): pl.pallas_call(functools.partial(fused_kernel, devices, 1.0 / math.sqrt(s...  66.9 us
    unnamed x10, local copies, waits for them, and re-layouts  4.32 us

profile of v1, /device:TPU:0, one launch (start us, length us, event | category | flops | bytes accessed | tf_op | source)
XLA Modules:
  0.0 71.9 jit_solution(7726118809243845252)
XLA Ops:
  0.6 66.9 %shard_map.165 = (f32[128,512]{1,0:T(8,128)}, f32[128,512]{1,0:T(8,128)}, f32[256,128]{1,0:T(8,128)}, f32[256,128]{1,0:T(8,128)}) custom-call(f32[128,512]{1,0:T(8,128)} %x_ref.1, f32[256,128]{1,0:T(8,128)} %vw_ref.1, f32[256,128]{1,0:T(8,128)} %qw_ref.1, f32[128,512]{1,0:T(8,128)} %f_ref.1, f32[128,512]{1,0:T(8,128)} %g_ref.1, ...), custom_call_target="tpu_custom_call" | custom-call | tf_op jit(solution)/shard_map/pallas_call | solution.py:503
  67.5 0.0 copy-start
  67.5 1.7 %copy.22 = f32[128,512]{1,0:T(8,128)} copy(f32[128,512]{1,0:T(8,128)} %get-tuple-element.8) | data formatting | bytes 524288
  69.3 0.0 copy-done
  69.3 0.0 copy-start.2
  69.3 0.7 copy.23
  70.0 0.3 copy-done.2
  70.3 0.0 copy-start.1
  70.3 0.7 copy.24
  70.9 0.3 copy-done.1
  71.2 0.7 copy.25
Async XLA Ops:
  67.5 1.7 %copy-start = (f32[128,512]{1,0:T(8,128)S(1)}, f32[128,512]{1,0:T(8,128)}, u32[]{:S(2)}) copy-start(f32[128,512]{1,0:T(8,128)} %get-tuple-element.9) | copy-start | bytes 786436
  69.3 1.0 %copy-start.2 = (f32[256,128]{1,0:T(8,128)S(1)}, f32[256,128]{1,0:T(8,128)}, u32[]{:S(2)}) copy-start(f32[256,128]{1,0:T(8,128)} %get-tuple-element.10) | copy-start | bytes 393220
  70.3 1.0 %copy-start.1 = (f32[256,128]{1,0:T(8,128)S(1)}, f32[256,128]{1,0:T(8,128)}, u32[]{:S(2)}) copy-start(f32[256,128]{1,0:T(8,128)} %get-tuple-element.11) | copy-start | bytes 393220

commit v2 on v1

--- a/solution.py
+++ b/solution.py
@@ -215,7 +215,8 @@
     b = np.arange(LANES, dtype=np.float64)
     phase = 2 * np.pi * np.outer(4 * k + 1, a) % (2 * np.pi * 4 * outer) / (4 * outer)
     small = np.concatenate([np.cos(phase), -np.sin(phase)], axis=0)
-    wide = np.kron(small, np.eye(GROUP)).astype(np.float32)
+    wide = np.repeat(small, GROUP, axis=0).astype(np.float32)
+    tall = (np.repeat(small.T, GROUP, axis=0) / seq_length).astype(np.float32)
     angle = 2 * np.pi * np.repeat(np.outer(4 * k + 1, b), GROUP, axis=0) / (4 * seq_length)
     turn = np.stack([np.cos(angle), np.sin(angle)]).astype(np.float32)
     inner = 2 * np.pi * (np.outer(b, b) % LANES) / LANES
@@ -224,7 +225,7 @@
     back = np.block([[c, s], [-s, c]]).astype(np.float32)
     return (
         *split_table(wide),
-        *split_table(np.ascontiguousarray(wide.T) / np.float32(seq_length)),
+        *split_table(tall),
         *split_table(ahead),
         *split_table(back),
         turn,
@@ -243,58 +244,48 @@
     return dot(first[0], second[0]) + (dot(first[0], second[1]) + dot(first[1], second[0]))
 
 
-def fused_kernel(
-    devices,
-    scale,
-    x_ref,
-    vw_ref,
-    qw_ref,
-    f_ref,
-    g_ref,
-    wide_h,
-    wide_l,
-    tall_h,
-    tall_l,
-    ahead_h,
-    ahead_l,
-    back_h,
-    back_l,
-    turn_ref,
-    ig_out,
-    fg_out,
-    vg_out,
-    qg_out,
-    other_x,
-    out_block,
-    send_sig,
-    in_sig,
-    spec,
-    out_sig,
-    ret_sig,
-    part,
-    scat,
-    red,
-    gath,
-    ig_send,
-    ig_recv,
-    ssem,
-    rsem,
-    csend,
-    crecv,
-):
+def spread(small_ref, out_ref):
+    rows, cols = out_ref.shape
+    inner = small_ref.shape[1]
+    pick = lax.broadcasted_iota(jnp.int32, (inner, cols), 1) // GROUP
+    own = lax.broadcasted_iota(jnp.int32, (inner, cols), 0)
+    picks = jnp.where(pick == own, 1.0, 0.0).astype(jnp.bfloat16)
+    row_lane = lax.broadcasted_iota(jnp.int32, (rows, cols), 0) % GROUP
+    col_lane = lax.broadcasted_iota(jnp.int32, (rows, cols), 1) % GROUP
+    full = lax.dot_general(small_ref[...], picks, NN, preferred_element_type=jnp.float32)
+    out_ref[...] = jnp.where(row_lane == col_lane, full, 0.0).astype(jnp.bfloat16)
+
+
+def fused_kernel(devices, scale, *refs):
+    x_hbm, vw_hbm, qw_hbm, f_hbm, g_hbm = refs[:5]
+    table_hbm = refs[5:14]
+    ig_out, fg_out, vg_out, qg_out = refs[14:18]
+    x_ref, vw_ref, qw_ref, g_ref = refs[18:22]
+    small_refs = refs[22:26]
+    ahead_h, ahead_l, back_h, back_l, turn_ref = refs[26:31]
+    wide_h, wide_l, tall_h, tall_l = refs[31:35]
+    other_x, send_sig, in_sig, spec, out_sig, ret_sig, part, scat, red, gath = refs[35:45]
+    ig_send, ig_recv, ssem, rsem, csend, crecv, lsem, osem = refs[45:]
     me = lax.axis_index("seq")
     chan = lax.axis_index("chan")
     half, width = x_ref.shape
     pieces = width // LANES
     rows = 2 * half // devices
 
+    def peer_of(i):
+        peer, bit = me, 1
+        while bit < devices:
+            peer = peer + (i // bit) % 2 * (1 - 2 * (me // bit % 2)) * bit
+            bit *= 2
+        return peer
+
     barrier = pltpu.get_barrier_semaphore()
 
     def greet(i, carry):
         pl.semaphore_signal(
             barrier,
             inc=1,
-            device_id={"seq": lax.rem(me + i, devices)},
+            device_id={"seq": peer_of(devices - i)},
             device_id_type=pl.DeviceIdType.MESH,
         )
         return carry
@@ -303,6 +294,24 @@
     pl.semaphore_signal(
         barrier, inc=1, device_id={"chan": 1 - chan}, device_id_type=pl.DeviceIdType.MESH
     )
+
+    loads = [
+        pltpu.make_async_copy(src, dst, lsem.at[at])
+        for at, (src, dst) in enumerate(
+            zip(
+                (x_hbm, vw_hbm, qw_hbm, g_hbm, *table_hbm),
+                (x_ref, vw_ref, qw_ref, g_ref, *small_refs)
+                + (ahead_h, ahead_l, back_h, back_l, turn_ref),
+            )
+        )
+    ]
+    for load in loads:
+        load.start()
+    own_f = pl.ds(pl.multiple_of(me * GROUP, GROUP), GROUP)
+    keep_f = pltpu.make_async_copy(f_hbm.at[own_f, :], in_sig.at[0, me], lsem.at[len(loads)])
+    keep_f.start()
+    for load in loads[:3]:
+        load.wait()
 
     own_rows = pl.ds(pl.multiple_of(chan * half, half), half)
     other_rows = pl.ds(pl.multiple_of((1 - chan) * half, half), half)
@@ -324,12 +333,13 @@
 
     def each(slot, src_of, dst_of, what):
         def step(i, carry):
-            peer = lax.rem(me + i, devices)
+            index = devices - i
+            peer = peer_of(index)
             copy = pltpu.make_async_remote_copy(
                 src_ref=src_of(peer),
                 dst_ref=dst_of(),
-                send_sem=ssem.at[slot, i],
-                recv_sem=rsem.at[slot, i],
+                send_sem=ssem.at[slot, index],
+                recv_sem=rsem.at[slot, index],
                 device_id={"seq": peer},
                 device_id_type=pl.DeviceIdType.MESH,
             )
@@ -342,7 +352,7 @@
         return pl.ds(pl.multiple_of(peer * count, count), count)
 
     def out_way(slot, what):
-        src = f_ref if slot == 0 else send_sig.at[slot - 1]
+        src = f_hbm if slot == 0 else send_sig.at[slot - 1]
         each(slot, lambda p: src.at[group_rows(p, GROUP), :], lambda: in_sig.at[slot, me], what)
 
     def back_way(slot, what):
@@ -369,10 +379,9 @@
             what,
         )
 
-    give_x = exchange(0, x_ref, other_x)
+    give_x = exchange(0, x_hbm, other_x)
     give_x.start()
     out_way(0, "start")
-    in_sig[0, me] = f_ref[group_rows(me, GROUP), :]
     give_x.wait()
 
     far_x = split(other_x[...])
@@ -380,10 +389,16 @@
     out_way(1, "start")
     in_sig[1, me] = send_sig[0, group_rows(me, GROUP), :]
     query_proj = partial_query + dot3(split(qw_ref[other_rows, :].T), far_x)
+    loads[3].wait()
     send_sig[1] = g_ref[...] * query_proj
     out_way(2, "start")
     in_sig[2, me] = send_sig[1, group_rows(me, GROUP), :]
 
+    for load in loads[4:]:
+        load.wait()
+    for small_ref, out_ref in zip(small_refs, (wide_h, wide_l, tall_h, tall_l)):
+        spread(small_ref, out_ref)
+    keep_f.wait()
     wide = (wide_h[...], wide_l[...])
     tall = (tall_h[...], tall_l[...])
     ahead = (ahead_h[...], ahead_l[...])
@@ -422,6 +437,8 @@
             [real * cosine - imag * sine, imag * cosine + real * sine], axis=0
         )
         signal = dot3(tall, split(turned))
+        if slot == 2:
+            signal = signal * scale
         for target in range(devices):
             for piece in range(pieces):
                 at = (target * pieces + piece) * GROUP
@@ -476,18 +493,29 @@
     near_grad = near_grad + dot3(split(vw_ref[own_rows, :]), grad_value)
     reduce(1)
     give_ig.wait()
-    ig_out[...] = near_grad + ig_recv[...]
+    ig_recv[...] = near_grad + ig_recv[...]
+    stores = [pltpu.make_async_copy(ig_recv, ig_out, osem.at[0])]
+    stores[0].start()
     back_way(2, "wait_recv")
-    fg_out[...] = ret_sig[2] * scale
+    stores.append(pltpu.make_async_copy(ret_sig.at[2], fg_out, osem.at[1]))
+    stores[1].start()
     for slot, out in ((0, qg_out), (1, vg_out)):
         gather(slot, "wait_recv")
-        out[...] = gath[slot]
+        stores.append(pltpu.make_async_copy(gath.at[slot], out, osem.at[2 + slot]))
+        stores[-1].start()
     for slot in range(3):
         out_way(slot, "wait_send")
         back_way(slot, "wait_send")
     for slot in range(2):
         scatter(slot, "wait_send")
         gather(slot, "wait_send")
+    for store in stores:
+        store.wait()
+
+
+def finish_kernel(*refs):
+    for source, target in zip(refs[:4], refs[4:]):
+        target[...] = source[...]
 
 
 def fused_device(inputs, value_weight, query_weight, filters, grad_out):
@@ -498,21 +526,32 @@
     rows = depth // devices
     tables = transform_tables(seq_length)
     count = seq_length // LANES * GROUP
+    tables = [jnp.asarray(t) for t in tables]
+    hbm = pl.BlockSpec(memory_space=pl.ANY)
     vmem = pl.BlockSpec(memory_space=pltpu.VMEM)
-    f32 = jnp.float32
-    ig, fg, vg, qg = pl.pallas_call(
+    f32, bf16 = jnp.float32, jnp.bfloat16
+    outs = (
+        jax.ShapeDtypeStruct((half, width), f32),
+        jax.ShapeDtypeStruct((half, width), f32),
+        jax.ShapeDtypeStruct((depth, half), f32),
+        jax.ShapeDtypeStruct((depth, half), f32),
+    )
+    results = pl.pallas_call(
         functools.partial(fused_kernel, devices, 1.0 / math.sqrt(seq_length)),
-        out_shape=(
-            jax.ShapeDtypeStruct((half, width), f32),
-            jax.ShapeDtypeStruct((half, width), f32),
-            jax.ShapeDtypeStruct((depth, half), f32),
-            jax.ShapeDtypeStruct((depth, half), f32),
-        ),
-        in_specs=[vmem] * (5 + len(tables)),
-        out_specs=(vmem,) * 4,
+        out_shape=outs,
+        in_specs=[hbm] * (5 + len(tables)),
+        out_specs=(hbm,) * 4,
         scratch_shapes=[
             pltpu.VMEM((half, width), f32),
-            pltpu.VMEM((GROUP, LANES), f32),
+            pltpu.VMEM((depth, half), f32),
+            pltpu.VMEM((depth, half), f32),
+            pltpu.VMEM((half, width), f32),
+            *(pltpu.VMEM(t.shape, t.dtype) for t in tables),
+            pltpu.VMEM((2 * count, count), bf16),
+            pltpu.VMEM((2 * count, count), bf16),
+            pltpu.VMEM((count, 2 * count), bf16),
+            pltpu.VMEM((count, 2 * count), bf16),
+            pltpu.VMEM((half, width), f32),
             pltpu.VMEM((2, half, width), f32),
             pltpu.VMEM((3, devices, GROUP, width), f32),
             pltpu.VMEM((3, count, 2 * LANES), f32),
@@ -528,12 +567,18 @@
             pltpu.SemaphoreType.DMA((10, devices)),
             pltpu.SemaphoreType.DMA((2,)),
             pltpu.SemaphoreType.DMA((2,)),
+            pltpu.SemaphoreType.DMA((5 + len(tables),)),
+            pltpu.SemaphoreType.DMA((4,)),
         ],
         compiler_params=pltpu.CompilerParams(
-            collective_id=0, has_side_effects=True, vmem_limit_bytes=56 * 1024 * 1024
+            collective_id=0, has_side_effects=True, vmem_limit_bytes=60 * 1024 * 1024
         ),
-    )(inputs, value_weight, query_weight, filters, grad_out, *(jnp.asarray(t) for t in tables))
-    return ig, fg, vg, qg
+    )(inputs, value_weight, query_weight, filters, grad_out, *tables)
+    return tuple(
+        pl.pallas_call(
+            finish_kernel, out_shape=outs, in_specs=[vmem] * 4, out_specs=(vmem,) * 4
+        )(*results)
+    )
 
 
 def on_device(inputs, value_weight, query_weight, filters, grad_out):
@@ -545,6 +590,7 @@
         and lax.axis_size("chan") == 2
         and width % LANES == 0
         and channel_count % LANES == 0
+        and devices & (devices - 1) == 0
         and value_weight.shape[0] % (GROUP * devices) == 0
     )
     body = fused_device if fits else per_device

time: 72 us -> 63.7 us (0.88)
  local copies, waits for them, and re-layouts: 4.32 us -> 0 us
  Pallas kernels: 66.9 us -> 62.9 us
    pallas_call x1, Pallas kernels: 66.9 us -> 61 us  [fused_device(): pl.pallas_call(functools.partial(fused_kernel, devices, 1.0 / math.sqrt(s...]
    unnamed x10 -> x0, local copies, waits for them, and re-layouts: 4.32 us -> none
    pallas_call x0 -> x1, Pallas kernels: none -> 1.99 us  [fused_device(): pl.pallas_call(finish_kernel, out_shape=outs, in_specs=[vmem] * 4, out_sp...]
where the time goes in v2:
time: 63.7 us; the launch traced here: 63.6 us
  Pallas kernels  62.9 us (99%)
  between operations  0.64 us (1%)
    pallas_call x1, Pallas kernels, fused_device(): pl.pallas_call(functools.partial(fused_kernel, devices, 1.0 / math.sqrt(s...  61 us
    pallas_call x1, Pallas kernels, fused_device(): pl.pallas_call(finish_kernel, out_shape=outs, in_specs=[vmem] * 4, out_sp...  1.99 us

profile of v2, /device:TPU:0, one launch (start us, length us, event | category | flops | bytes accessed | tf_op | source)
XLA Modules:
  0.0 63.6 jit_solution(4624937871414106557)
XLA Ops:
  0.6 61.0 %shard_map.165 = (f32[128,512]{1,0:T(8,128)}, f32[128,512]{1,0:T(8,128)}, f32[256,128]{1,0:T(8,128)}, f32[256,128]{1,0:T(8,128)}) custom-call(f32[128,512]{1,0:T(8,128)} %refs_0_.1, f32[256,128]{1,0:T(8,128)} %refs_1_.1, f32[256,128]{1,0:T(8,128)} %refs_2_.1, f32[128,512]{1,0:T(8,128)} %refs_3_.1, f32[128,512]{1,0:T(8,128)} %refs_4_.1, ...), custom_call_target="tpu_custom_call" | custom-call | tf_op jit(solution)/shard_map/pallas_call | solution.py:539
  61.6 2.0 %shard_map.166 = (f32[128,512]{1,0:T(8,128)}, f32[128,512]{1,0:T(8,128)}, f32[256,128]{1,0:T(8,128)}, f32[256,128]{1,0:T(8,128)}) custom-call(f32[128,512]{1,0:T(8,128)} %get-tuple-element.8.refs_0_, f32[128,512]{1,0:T(8,128)} %get-tuple-element.9.refs_1_, f32[256,128]{1,0:T(8,128)} %get-tuple-element.10.refs_2_, f32[256,128]{1,0:T(8,128)} %get-tuple-element.11.refs_3_), custom_call_target="tpu_custom_call" | custom-call | tf_op jit(solution)/shard_map/pallas_call | solution.py:578

commit v3 on v2

--- a/solution.py
+++ b/solution.py
@@ -270,7 +270,10 @@
     chan = lax.axis_index("chan")
     half, width = x_ref.shape
     pieces = width // LANES
-    rows = 2 * half // devices
+    inner = 1 << (devices.bit_length() - 1) // 2
+    outer = devices // inner
+    rows = 2 * half // inner
+    me_inner, me_outer = me % inner, me // inner
 
     def peer_of(i):
         peer, bit = me, 1
@@ -331,9 +334,9 @@
             device_id_type=pl.DeviceIdType.MESH,
         )
 
-    def each(slot, src_of, dst_of, what):
+    def each(slot, src_of, dst_of, what, count=devices, stride=1):
         def step(i, carry):
-            index = devices - i
+            index = (count - i) * stride
             peer = peer_of(index)
             copy = pltpu.make_async_remote_copy(
                 src_ref=src_of(peer),
@@ -346,7 +349,7 @@
             getattr(copy, what)()
             return carry
 
-        lax.fori_loop(1, devices, step, 0)
+        lax.fori_loop(1, count, step, 0)
 
     def group_rows(peer, count):
         return pl.ds(pl.multiple_of(peer * count, count), count)
@@ -366,17 +369,29 @@
     def scatter(slot, what):
         each(
             6 + slot,
-            lambda p: part.at[slot, group_rows(p, rows), :],
-            lambda: scat.at[slot, me],
+            lambda p: part.at[slot, group_rows(p % inner, rows), :],
+            lambda: scat.at[slot, me_inner],
             what,
+            inner,
+        )
+
+    def swap(slot, what):
+        each(
+            8 + slot,
+            lambda p: red.at[slot, me_outer],
+            lambda: red.at[slot, me_outer],
+            what,
+            outer,
+            inner,
         )
 
     def gather(slot, what):
         each(
-            8 + slot,
-            lambda p: red.at[slot],
-            lambda: gath.at[slot, group_rows(me, rows), :],
+            10 + slot,
+            lambda p: gath.at[slot, group_rows(me_inner, rows), :],
+            lambda: gath.at[slot, group_rows(me_inner, rows), :],
             what,
+            inner,
         )
 
     give_x = exchange(0, x_hbm, other_x)
@@ -459,12 +474,10 @@
     restore(1, 2, True, 2)
 
     def weight_part(slot, grad):
-        near = dot3(own_x2, grad, NT)
-        far = dot3(far_x2, grad, NT)
-        part[slot, own_rows, :] = near
-        part[slot, other_rows, :] = far
+        part[slot, own_rows, :] = dot3(own_x2, grad, NT)
+        part[slot, other_rows, :] = dot3(far_x2, grad, NT)
         scatter(slot, "start")
-        scat[slot, me] = part[slot, group_rows(me, rows), :]
+        scat[slot, me_inner] = part[slot, group_rows(me_inner, rows), :]
 
     own_x2 = split(x_ref[...])
     far_x2 = split(other_x[...])
@@ -473,29 +486,38 @@
     weight_part(0, grad_query)
     near_grad = dot3(split(qw_ref[own_rows, :]), grad_query)
     far_grad = dot3(split(qw_ref[other_rows, :]), grad_query)
+
+    def reduce_inner(slot):
+        scatter(slot, "wait_recv")
+        total = scat[slot, 0]
+        for source in range(1, inner):
+            total = total + scat[slot, source]
+        red[slot, me_outer] = total
+        swap(slot, "start")
+
+    def reduce_outer(slot):
+        swap(slot, "wait_recv")
+        total = red[slot, 0]
+        for source in range(1, outer):
+            total = total + red[slot, source]
+        gath[slot, group_rows(me_inner, rows), :] = total * scale
+        gather(slot, "start")
+
+    reduce_inner(0)
     back_way(1, "wait_recv")
     grad_value = split(ret_sig[1])
+    weight_part(1, grad_value)
     ig_send[...] = far_grad + dot3(split(vw_ref[other_rows, :]), grad_value)
     give_ig = exchange(1, ig_send, ig_recv)
     give_ig.start()
-    weight_part(1, grad_value)
-
-    def reduce(slot):
-        scatter(slot, "wait_recv")
-        total = scat[slot, 0]
-        for source in range(1, devices):
-            total = total + scat[slot, source]
-        red[slot] = total * scale
-        gather(slot, "start")
-        gath[slot, group_rows(me, rows), :] = red[slot]
-
-    reduce(0)
+    reduce_inner(1)
     near_grad = near_grad + dot3(split(vw_ref[own_rows, :]), grad_value)
-    reduce(1)
+    reduce_outer(0)
     give_ig.wait()
     ig_recv[...] = near_grad + ig_recv[...]
     stores = [pltpu.make_async_copy(ig_recv, ig_out, osem.at[0])]
     stores[0].start()
+    reduce_outer(1)
     back_way(2, "wait_recv")
     stores.append(pltpu.make_async_copy(ret_sig.at[2], fg_out, osem.at[1]))
     stores[1].start()
@@ -508,6 +530,7 @@
         back_way(slot, "wait_send")
     for slot in range(2):
         scatter(slot, "wait_send")
+        swap(slot, "wait_send")
         gather(slot, "wait_send")
     for store in stores:
         store.wait()
@@ -523,7 +546,9 @@
     devices = lax.axis_size("seq")
     seq_length = width * devices
     depth = value_weight.shape[0]
-    rows = depth // devices
+    inner = 1 << (devices.bit_length() - 1) // 2
+    outer = devices // inner
+    rows = depth // inner
     tables = transform_tables(seq_length)
     count = seq_length // LANES * GROUP
     tables = [jnp.asarray(t) for t in tables]
@@ -558,13 +583,13 @@
             pltpu.VMEM((3, devices, GROUP, width), f32),
             pltpu.VMEM((3, half, width), f32),
             pltpu.VMEM((2, depth, half), f32),
-            pltpu.VMEM((2, devices, rows, half), f32),
-            pltpu.VMEM((2, rows, half), f32),
+            pltpu.VMEM((2, inner, rows, half), f32),
+            pltpu.VMEM((2, outer, rows, half), f32),
             pltpu.VMEM((2, depth, half), f32),
             pltpu.VMEM((half, width), f32),
             pltpu.VMEM((half, width), f32),
-            pltpu.SemaphoreType.DMA((10, devices)),
-            pltpu.SemaphoreType.DMA((10, devices)),
+            pltpu.SemaphoreType.DMA((12, devices)),
+            pltpu.SemaphoreType.DMA((12, devices)),
             pltpu.SemaphoreType.DMA((2,)),
             pltpu.SemaphoreType.DMA((2,)),
             pltpu.SemaphoreType.DMA((5 + len(tables),)),

time: 63.7 us -> 60.6 us (0.951)
  Pallas kernels: 62.9 us -> 59.8 us
    pallas_call x1, Pallas kernels: 61 us -> 57.8 us  [fused_device(): pl.pallas_call(functools.partial(fused_kernel, devices, 1.0 / math.sqrt(s...]
where the time goes in v3:
time: 60.6 us; the launch traced here: 60.5 us
  Pallas kernels  59.8 us (99%)
  between operations  0.64 us (1%)
    pallas_call x1, Pallas kernels, fused_device(): pl.pallas_call(functools.partial(fused_kernel, devices, 1.0 / math.sqrt(s...  57.8 us
    pallas_call x1, Pallas kernels, fused_device(): pl.pallas_call(finish_kernel, out_shape=outs, in_specs=[vmem] * 4, out_sp...  1.99 us

profile of v3, /device:TPU:0, one launch (start us, length us, event | category | flops | bytes accessed | tf_op | source)
XLA Modules:
  0.0 60.5 jit_solution(15533864019813594220)
XLA Ops:
  0.6 57.8 %shard_map.165 = (f32[128,512]{1,0:T(8,128)}, f32[128,512]{1,0:T(8,128)}, f32[256,128]{1,0:T(8,128)}, f32[256,128]{1,0:T(8,128)}) custom-call(f32[128,512]{1,0:T(8,128)} %refs_0_.1, f32[256,128]{1,0:T(8,128)} %refs_1_.1, f32[256,128]{1,0:T(8,128)} %refs_2_.1, f32[128,512]{1,0:T(8,128)} %refs_3_.1, f32[128,512]{1,0:T(8,128)} %refs_4_.1, ...), custom_call_target="tpu_custom_call" | custom-call | tf_op jit(solution)/shard_map/pallas_call | solution.py:564
  58.5 2.0 %shard_map.166 = (f32[128,512]{1,0:T(8,128)}, f32[128,512]{1,0:T(8,128)}, f32[256,128]{1,0:T(8,128)}, f32[256,128]{1,0:T(8,128)}) custom-call(f32[128,512]{1,0:T(8,128)} %get-tuple-element.8.refs_0_, f32[128,512]{1,0:T(8,128)} %get-tuple-element.9.refs_1_, f32[256,128]{1,0:T(8,128)} %get-tuple-element.10.refs_2_, f32[256,128]{1,0:T(8,128)} %get-tuple-element.11.refs_3_), custom_call_target="tpu_custom_call" | custom-call | tf_op jit(solution)/shard_map/pallas_call | solution.py:603

commit v4 on v3

--- a/solution.py
+++ b/solution.py
@@ -265,7 +265,7 @@
     ahead_h, ahead_l, back_h, back_l, turn_ref = refs[26:31]
     wide_h, wide_l, tall_h, tall_l = refs[31:35]
     other_x, send_sig, in_sig, spec, out_sig, ret_sig, part, scat, red, gath = refs[35:45]
-    ig_send, ig_recv, ssem, rsem, csend, crecv, lsem, osem = refs[45:]
+    ig_send, ig_recv, ssem, rsem, csend, crecv, lsem = refs[45:]
     me = lax.axis_index("seq")
     chan = lax.axis_index("chan")
     half, width = x_ref.shape
@@ -514,17 +514,13 @@
     near_grad = near_grad + dot3(split(vw_ref[own_rows, :]), grad_value)
     reduce_outer(0)
     give_ig.wait()
-    ig_recv[...] = near_grad + ig_recv[...]
-    stores = [pltpu.make_async_copy(ig_recv, ig_out, osem.at[0])]
-    stores[0].start()
+    ig_out[...] = near_grad + ig_recv[...]
     reduce_outer(1)
     back_way(2, "wait_recv")
-    stores.append(pltpu.make_async_copy(ret_sig.at[2], fg_out, osem.at[1]))
-    stores[1].start()
+    fg_out[...] = ret_sig[2]
     for slot, out in ((0, qg_out), (1, vg_out)):
         gather(slot, "wait_recv")
-        stores.append(pltpu.make_async_copy(gath.at[slot], out, osem.at[2 + slot]))
-        stores[-1].start()
+        out[...] = gath[slot]
     for slot in range(3):
         out_way(slot, "wait_send")
         back_way(slot, "wait_send")
@@ -532,13 +528,17 @@
         scatter(slot, "wait_send")
         swap(slot, "wait_send")
         gather(slot, "wait_send")
+
+
+def finish_kernel(*refs):
+    stores = [
+        pltpu.make_async_copy(source, target, refs[8].at[at])
+        for at, (source, target) in enumerate(zip(refs[:4], refs[4:8]))
+    ]
+    for store in stores:
+        store.start()
     for store in stores:
         store.wait()
-
-
-def finish_kernel(*refs):
-    for source, target in zip(refs[:4], refs[4:]):
-        target[...] = source[...]
 
 
 def fused_device(inputs, value_weight, query_weight, filters, grad_out):
@@ -552,7 +552,7 @@
     tables = transform_tables(seq_length)
     count = seq_length // LANES * GROUP
     tables = [jnp.asarray(t) for t in tables]
-    hbm = pl.BlockSpec(memory_space=pl.ANY)
+    hbm = pl.BlockSpec(memory_space=pltpu.HBM)
     vmem = pl.BlockSpec(memory_space=pltpu.VMEM)
     f32, bf16 = jnp.float32, jnp.bfloat16
     outs = (
@@ -563,9 +563,9 @@
     )
     results = pl.pallas_call(
         functools.partial(fused_kernel, devices, 1.0 / math.sqrt(seq_length)),
-        out_shape=outs,
+        out_shape=tuple(pltpu.VMEM(out.shape, out.dtype) for out in outs),
         in_specs=[hbm] * (5 + len(tables)),
-        out_specs=(hbm,) * 4,
+        out_specs=(vmem,) * 4,
         scratch_shapes=[
             pltpu.VMEM((half, width), f32),
             pltpu.VMEM((depth, half), f32),
@@ -593,7 +593,6 @@
             pltpu.SemaphoreType.DMA((2,)),
             pltpu.SemaphoreType.DMA((2,)),
             pltpu.SemaphoreType.DMA((5 + len(tables),)),
-            pltpu.SemaphoreType.DMA((4,)),
         ],
         compiler_params=pltpu.CompilerParams(
             collective_id=0, has_side_effects=True, vmem_limit_bytes=60 * 1024 * 1024
@@ -601,8 +600,12 @@
     )(inputs, value_weight, query_weight, filters, grad_out, *tables)
     return tuple(
         pl.pallas_call(
-            finish_kernel, out_shape=outs, in_specs=[vmem] * 4, out_specs=(vmem,) * 4
-        )(*results)
+            finish_kernel,
+            out_shape=outs,
+            in_specs=[vmem] * 4,
+            out_specs=(hbm,) * 4,
+            scratch_shapes=[pltpu.SemaphoreType.DMA((4,))],
+        )(*(pltpu.with_memory_space_constraint(r, pltpu.VMEM) for r in results))
     )
 
 

time: 60.6 us -> 59.5 us (0.982)
  Pallas kernels: 59.8 us -> 58.8 us
    pallas_call x1, Pallas kernels: 1.99 us -> 0.91 us  [fused_device(): pl.pallas_call(finish_kernel, out_shape=outs, in_specs=[vmem] * 4, out_sp...]
where the time goes in v4:
time: 59.5 us; the launch traced here: 59.4 us
  Pallas kernels  58.8 us (99%)
  between operations  0.64 us (1%)
    pallas_call x1, Pallas kernels, fused_device(): pl.pallas_call(functools.partial(fused_kernel, devices, 1.0 / math.sqrt(s...  57.8 us

profile of v4, /device:TPU:0, one launch (start us, length us, event | category | flops | bytes accessed | tf_op | source)
XLA Modules:
  0.0 59.4 jit_solution(12985259055940559595)
XLA Ops:
  0.6 57.8 %shard_map.165 = (f32[128,512]{1,0:T(8,128)S(1)}, f32[128,512]{1,0:T(8,128)S(1)}, f32[256,128]{1,0:T(8,128)S(1)}, f32[256,128]{1,0:T(8,128)S(1)}) custom-call(f32[128,512]{1,0:T(8,128)} %refs_0_.1, f32[256,128]{1,0:T(8,128)} %refs_1_.1, f32[256,128]{1,0:T(8,128)} %refs_2_.1, f32[128,512]{1,0:T(8,128)} %refs_3_.1, f32[128,512]{1,0:T(8,128)} %refs_4_.1, ...), custom_call_target="tpu_custom_call" | custom-call | tf_op jit(solution)/shard_map/pallas_call | solution.py:564
  58.5 0.9 %shard_map.166 = (f32[128,512]{1,0:T(8,128)}, f32[128,512]{1,0:T(8,128)}, f32[256,128]{1,0:T(8,128)}, f32[256,128]{1,0:T(8,128)}) custom-call(f32[128,512]{1,0:T(8,128)S(1)} %get-tuple-element.8.refs_0_, f32[128,512]{1,0:T(8,128)S(1)} %get-tuple-element.9.refs_1_, f32[256,128]{1,0:T(8,128)S(1)} %get-tuple-element.10.refs_2_, ...), custom_call_target="tpu_custom_call" | custom-call | tf_op jit(solution)/shard_map/pallas_call | solution.py:602
